TPU v7x, 32 devices: a whole 2x2x4 slice. The times are simulated.
32 devices in a mesh: row: 16 (over z, x, core), col: 2 (over y).
Axes of the slice: x: 2, y: 2, z: 4, core: 2. Of those that a mesh axis runs over, the one named last changes fastest.
Arguments:
- base_velocity: bfloat16 [3, 512, 256, 384], P(None, 'row', 'col'), may hold values from -6 to 6
- velocity_step: bfloat16 [3, 512, 256, 384], P(None, 'row', 'col'), may hold values from -6 to 6
- adjoint_velocity: bfloat16 [3, 512, 256, 384], P(None, 'row', 'col'), may hold values from -6 to 6
- increment_weight: float32 [1], replicated, may hold values from 0.3 to 0.9
- streamwise_first: bfloat16 [3, 128, 128], replicated, may hold values from -0.3125 to 0.3125
- streamwise_second: bfloat16 [3, 128, 128], replicated, may hold values from -0.3125 to 0.3125
- normal_first: bfloat16 [512, 512], replicated, may hold values from -0.25 to 0.25
- normal_second: bfloat16 [512, 512], replicated, may hold values from -0.25 to 0.25
- spanwise_first: bfloat16 [256, 256], replicated, may hold values from -0.375 to 0.375
- spanwise_second: bfloat16 [256, 256], replicated, may hold values from -0.375 to 0.375
- wall_profile: float32 [2, 512], P(None, 'row'), may hold values from 0.5 to 1.5
Outputs:
- adjoint_tendency: bfloat16 [3, 512, 256, 384], P(None, 'row', 'col')
All inputs are finite; a program needn't handle non-finite values.
Results may differ from a plain program's by a relative error of at most 0.012.
Values may be sent and summed in bfloat16 or wider, within the bound.
No kernel may reach another device: no remote copies, remote signals or barrier semaphores. Data moves between devices by JAX's collectives and lax.ppermute only.
A program may use at most 448 MiB of HBM per device.

v0:
```python
import jax
import jax.numpy as jnp
from jax import lax
from jax.sharding import PartitionSpec as P


def along_stream(field, operators):
    block_width = operators[0].shape[1]
    block_count = field.shape[-1] // block_width
    tiles = field.reshape(field.shape[:-1] + (block_count, block_width))
    joined = jnp.concatenate([blocks[k] for blocks in operators for k in range(3)], axis=1)
    product = jnp.dot(tiles, joined, preferred_element_type=jnp.float32)
    results = []
    for number in range(len(operators)):
        start = 3 * number * block_width
        lower = product[..., start : start + block_width]
        middle = product[..., start + block_width : start + 2 * block_width]
        upper = product[..., start + 2 * block_width : start + 3 * block_width]
        combined = jnp.roll(lower, 1, axis=-2) + middle + jnp.roll(upper, -1, axis=-2)
        results.append(combined.reshape(field.shape))
    return results


def normal_products(speed, adjoint, first_op, second_op):
    slope_speed = jnp.einsum("wy,cyp->cwp", first_op, speed, preferred_element_type=jnp.float32)
    stacked = jnp.concatenate([first_op, second_op], axis=0)
    both = jnp.einsum("wy,cyp->cwp", stacked, adjoint, preferred_element_type=jnp.float32)
    lines = first_op.shape[0]
    return (slope_speed, both[:, :lines], both[:, lines:])


def span_products(speed, adjoint, first_op, second_op):
    slope_speed = jnp.einsum("vz,cyzx->cyvx", first_op, speed, preferred_element_type=jnp.float32)
    stacked = jnp.concatenate([first_op, second_op], axis=0)
    both = jnp.einsum("vz,cyzx->cyvx", stacked, adjoint, preferred_element_type=jnp.float32)
    planes = first_op.shape[0]
    return (slope_speed, both[:, :, :planes], both[:, :, planes:])


def component_mask(which, ndim):
    return (jnp.arange(3) == which).astype(jnp.float32).reshape((3,) + (1,) * (ndim - 1))


def adjoint_terms(velocity, adjoint, slope_velocity, slope_adjoint, curve_adjoint, direction):
    cross = jnp.sum(adjoint.astype(jnp.float32) * slope_velocity, axis=0)
    advect = velocity[direction].astype(jnp.float32)[None] * slope_adjoint
    return curve_adjoint - advect + component_mask(direction, adjoint.ndim) * cross[None]


def per_device(
    base_velocity,
    velocity_step,
    adjoint_velocity,
    increment_weight,
    streamwise_first,
    streamwise_second,
    normal_first,
    normal_second,
    spanwise_first,
    spanwise_second,
    wall_profile,
):
    velocity = (
        base_velocity.astype(jnp.float32) + increment_weight[0] * velocity_step.astype(jnp.float32)
    ).astype(jnp.bfloat16)
    (slope_speed,) = along_stream(velocity, [streamwise_first])
    slope_adjoint, curve_adjoint = along_stream(
        adjoint_velocity, [streamwise_first, streamwise_second]
    )
    near = adjoint_terms(velocity, adjoint_velocity, slope_speed, slope_adjoint, curve_adjoint, 0)
    local_rows = velocity.shape[1]
    local_planes = velocity.shape[2]
    stream_cells = velocity.shape[3]
    flat_speed = velocity.reshape(3, local_rows, local_planes * stream_cells)
    flat_adjoint = adjoint_velocity.reshape(3, local_rows, local_planes * stream_cells)
    speed_lines, adjoint_lines = (
        lax.all_to_all(flat_speed, "row", split_axis=2, concat_axis=1, tiled=True),
        lax.all_to_all(flat_adjoint, "row", split_axis=2, concat_axis=1, tiled=True),
    )
    normal_speed, normal_adjoint, normal_curve = normal_products(
        speed_lines, adjoint_lines, normal_first, normal_second
    )
    normal_term = adjoint_terms(
        speed_lines, adjoint_lines, normal_speed, normal_adjoint, normal_curve, 1
    ).astype(jnp.bfloat16)
    strip = jnp.stack([normal_speed[0, 0], normal_speed[0, -1]]).astype(jnp.bfloat16)
    wall_shear = lax.all_gather(strip, "row", axis=1, tiled=True).reshape(
        2, local_planes, stream_cells
    )
    normal_home = lax.all_to_all(
        normal_term, "row", split_axis=1, concat_axis=2, tiled=True
    ).reshape(3, local_rows, local_planes, stream_cells)
    speed_span, adjoint_span = (
        lax.all_to_all(velocity, "col", split_axis=1, concat_axis=2, tiled=True),
        lax.all_to_all(adjoint_velocity, "col", split_axis=1, concat_axis=2, tiled=True),
    )
    span_speed, span_adjoint, span_curve = span_products(
        speed_span, adjoint_span, spanwise_first, spanwise_second
    )
    span_term = adjoint_terms(
        speed_span, adjoint_span, span_speed, span_adjoint, span_curve, 2
    ).astype(jnp.bfloat16)
    span_home = lax.all_to_all(span_term, "col", split_axis=2, concat_axis=1, tiled=True)
    far_terms = (normal_home.astype(jnp.float32) + span_home.astype(jnp.float32)).astype(
        jnp.bfloat16
    )
    (shear_slope,) = along_stream(wall_shear, [streamwise_first])
    forcing = (
        wall_profile[0][:, None, None] * shear_slope[0][None]
        + wall_profile[1][:, None, None] * shear_slope[1][None]
    )
    total = near + far_terms.astype(jnp.float32) + component_mask(0, 4) * forcing[None]
    return total.astype(jnp.bfloat16)


def solution(mesh):
    placed = (
        P(None, "row", "col", None),
        P(None, "row", "col", None),
        P(None, "row", "col", None),
        P(),
        P(),
        P(),
        P(),
        P(),
        P(),
        P(),
        P(None, "row"),
    )
    return jax.shard_map(
        per_device,
        mesh=mesh,
        in_specs=placed,
        out_specs=P(None, "row", "col", None),
        check_vma=False,
    )
```

profile of v0, /device:TPU:13, one launch (start us, length us, event | category | flops | bytes accessed | tf_op | source)
XLA Modules:
  0.0 1365.6 jit_solution(14723358383659704467)
XLA Ops:
  0.0 9.1 copy.205
  9.1 7.5 all-to-all-start.3
  16.6 12.6 copy.186
  29.2 12.6 copy.185
  42.5 12.5 add_convert_fusion.2
  55.0 8.5 copy.207
  63.5 55.0 %all-to-all-done.3 = bf16[3,32,128,384]{3,2,0,1:T(8,128)(2,1)} async-done(((bf16[3,32,128,384]{3,2,0,1:T(8,128)(2,1)}), bf16[3,32,128,384]{3,2,0,1:T(8,128)(2,1)}, u32[]{:S(2)}, u32[]{:S(2)}) %all-to-all-start.3) | async-done | bytes 9437216 | tf_op jit(solution)/shard_map/all_to_all | solution.py:95
  118.5 8.5 all-to-all-start.4
  127.0 81.2 %copy.232 = bf16[3,32,128,384]{1,0,3,2:T(4,128)(2,1)} copy(bf16[3,32,128,384]{2,3,1,0:T(8,128)(2,1)} %add_convert_fusion.2) | data formatting | bytes 18874368 | tf_op jit(solution)/shard_map/reshape | solution.py:74
  208.2 36.1 %reshape.104 = bf16[16,2,147456]{2,1,0:T(2,128)(2,1)} reshape(bf16[49152,3,32]{2,1,0:T(4,128)(2,1)} %bitcast.130) | data formatting | bytes 18874368
  244.3 7.7 all-to-all-start.1
  252.0 48.7 %copy.195 = bf16[3,32,128,384]{1,0,3,2:T(4,128)(2,1)} copy(bf16[3,32,128,384]{3,2,1,0:T(8,128)(2,1)} %param.13) | data formatting | bytes 18874368 | tf_op args[2]
  300.7 36.1 %reshape.102 = bf16[16,2,147456]{2,1,0:T(2,128)(2,1)} reshape(bf16[49152,3,32]{2,1,0:T(4,128)(2,1)} %bitcast.131) | data formatting | bytes 18874368
  336.8 117.9 %all-to-all-done.1 = bf16[16,2,147456]{2,1,0:T(2,128)(2,1)} async-done(((bf16[16,2,147456]{2,1,0:T(2,128)(2,1)}), bf16[16,2,147456]{2,1,0:T(2,128)(2,1)}, u32[]{:S(2)}, u32[]{:S(2)}) %all-to-all-start.1) | async-done | bytes 9437216 | tf_op jit(solution)/shard_map/all_to_all | solution.py:77
  454.7 7.7 all-to-all-start
  462.4 12.7 copy.183
  475.8 0.5 compare_convert_fusion.1
  476.4 40.9 %convolution_bitcast_fusion = f32[3,32,128,3,768]{2,4,3,1,0:T(8,128)} fusion(bf16[3,32,128,3,128]{2,4,3,1,0:T(8,128)(2,1)} %bitcast.132, bf16[128,768]{0,1:T(8,128)(2,1)S(1)} %bitcast_dynamic-update-slice_fusion), kind=kOutput, calls=%fused_computation | convolution fusion | flops 7247757312 | bytes 122880000 | tf_op jit(solution)/shard_map/dot_general | solution.py:12
  517.3 31.5 %fusion.31 = (f32[3,32,128,2,128]{2,4,3,1,0:T(8,128)}, f32[3,32,128,2,128]{2,4,3,1,0:T(8,128)}, f32[3,32,128,2,128]{2,4,3,1,0:T(8,128)}, f32[3,32,128,2,128]{2,4,3,1,0:T(8,128)}) fusion(f32[3,32,128,3,768]{2,4,3,1,0:T(8,128)} %convolution_bitcast_fusion), kind=kLoop, calls=%fused_computation.69 | loop fusion | bytes 100663296 | tf_op jit(solution)/shard_map/jit(_roll_static)/slice | solution.py:19
  548.9 9.1 copy.206
  558.0 12.6 copy.209
  570.6 2.4 slice.220
  573.1 3.3 convert.20
  576.3 12.7 fusion.9
  589.1 18.7 %convolution_bitcast_fusion.2 = f32[3,16,512,384]{3,2,1,0:T(8,128)} fusion(bf16[3,16,256,384]{3,2,1,0:T(8,128)(2,1)} %bitcast.134, bf16[256,256]{1,0:T(8,128)(2,1)S(1)} %copy-done.8, bf16[256,256]{1,0:T(8,128)(2,1)S(1)} %copy-done.1), kind=kOutput, calls=%fused_computation.28 | convolution fusion | flops 4832362496 | bytes 47448064 | tf_op jit(solution)/shard_map/vz,cyzx->cyvx/dot_general | solution.py:35
  607.8 19.0 %fusion.2 = bf16[3,16,256,384]{3,2,1,0:T(8,128)(2,1)} fusion(f32[3,16,512,384]{3,2,1,0:T(8,128)} %convolution_bitcast_fusion.2, f32[16,256,384]{2,1,0:T(8,128)} %fusion.9, f32[3]{0:T(128)S(1)} %compare_convert_fusion, f32[16,256,384]{2,1,0:T(8,128)S(1)} %bitcast.146), kind=kLoop, calls=%fused_computation.5 | loop fusion | flops 23592960 | bytes 59768844 | tf_op jit(solution)/shard_map/convert_element_type | solution.py:102
  626.7 12.8 copy.212
  639.6 35.8 %reshape.105 = bf16[49152,3,32]{2,1,0:T(4,128)(2,1)} reshape(bf16[16,2,147456]{2,1,0:T(2,128)(2,1)} %all-to-all-done.1) | data formatting | bytes 18874368
  675.4 58.5 %copy.234 = bf16[3,32,16,3072]{3,1,2,0:T(8,128)(2,1)} copy(bf16[3,32,16,3072]{1,0,3,2:T(4,128)(2,1)} %bitcast.126) | data formatting | bytes 18874368 | tf_op jit(solution)/shard_map/all_to_all | solution.py:77
  733.9 47.1 %copy.233 = bf16[3,32,16,3072]{3,2,1,0:T(8,128)(2,1)} copy(bf16[3,32,16,3072]{1,0,3,2:T(4,128)(2,1)} %bitcast.127) | data formatting | bytes 18874368 | tf_op jit(solution)/shard_map/all_to_all | solution.py:77
  781.0 7.3 all-to-all-start.5
  788.3 36.1 %reshape.103 = bf16[49152,3,32]{2,1,0:T(4,128)(2,1)} reshape(bf16[16,2,147456]{2,1,0:T(2,128)(2,1)} %all-to-all-done) | data formatting | bytes 18874368
  824.3 58.5 %copy.231 = bf16[3,32,16,3072]{3,1,2,0:T(8,128)(2,1)} copy(bf16[3,32,16,3072]{1,0,3,2:T(4,128)(2,1)} %bitcast.129) | data formatting | bytes 18874368 | tf_op jit(solution)/shard_map/all_to_all | solution.py:78
  882.8 2.8 slice_convert_fusion
  885.7 6.3 copy.201
  892.0 11.9 bitcast_convert_fusion
  903.9 13.1 fusion.10
  917.0 20.5 %convolution_bitcast_fusion.1 = f32[3,1024,3072]{2,1,0:T(8,128)} fusion(bf16[3,512,3072]{2,1,0:T(8,128)(2,1)} %bitcast.143, bf16[512,512]{1,0:T(8,128)(2,1)S(1)} %copy-done.13, bf16[512,512]{1,0:T(8,128)(2,1)S(1)} %copy-done), kind=kOutput, calls=%fused_computation.27 | convolution fusion | flops 9665773568 | bytes 48234496 | tf_op jit(solution)/shard_map/wy,cyp->cwp/dot_general | solution.py:27
  937.5 16.8 %fusion.5 = bf16[3,512,3072]{2,1,0:T(8,128)(2,1)S(1)} fusion(f32[3,1024,3072]{2,1,0:T(8,128)} %convolution_bitcast_fusion.1, f32[512,3072]{1,0:T(8,128)} %fusion.10, f32[3]{0:T(128)S(1)} %copy-done.12, f32[512,3072]{1,0:T(8,128)} %bitcast.144), kind=kLoop, calls=%fused_computation.9 | loop fusion | flops 23592960 | bytes 59768844 | tf_op jit(solution)/shard_map/convert_element_type | solution.py:85
  954.4 39.2 %copy.203 = bf16[3,512,3072]{2,0,1:T(4,128)(2,1)} copy(bf16[3,512,3072]{2,1,0:T(8,128)(2,1)S(1)} %fusion.5) | data formatting | bytes 18874368 | tf_op jit(solution)/shard_map/convert_element_type | solution.py:85
  993.6 6.5 all-to-all-start.2
  1000.1 16.0 %fusion.32 = (f32[3,32,128,1,128]{2,4,3,1,0:T(8,128)}, f32[3,32,128,1,128]{2,4,3,1,0:T(8,128)}, f32[3,32,128,1,128]{2,4,3,1,0:T(8,128)}, f32[3,32,128,1,128]{2,4,3,1,0:T(8,128)}) fusion(f32[3,32,128,3,768]{2,4,3,1,0:T(8,128)} %convolution_bitcast_fusion), kind=kLoop, calls=%fused_computation.70 | loop fusion | bytes 50331648 | tf_op jit(solution)/shard_map/jit(_roll_static)/slice | solution.py:19
  1016.1 50.3 %fusion.7 = (f32[3,32,128,3,128]{2,4,3,1,0:T(8,128)}, f32[3,32,128,3,128]{2,4,3,1,0:T(8,128)}) fusion(f32[3,32,128,3,768]{2,4,3,1,0:T(8,128)} %convolution_bitcast_fusion, f32[3,32,128,2,128]{2,4,3,1,0:T(8,128)} %get-tuple-element.8, f32[3,32,128,1,128]{2,4,3,1,0:T(8,128)} %get-tuple-element.12, f32[3,32,128,1,128]{2,4,3,1,0:T(8,128)} %get-tuple-element.11, ...), kind=kLoop, calls=%fused_computation.13 | loop fusion | flops 37748736 | bytes 150994944 | tf_op jit(solution)/shard_map/add | solution.py:19
  1066.3 18.7 %copy.189 = f32[3,32,128,384]{3,2,1,0:T(8,128)} copy(f32[3,32,128,384]{2,3,1,0:T(8,128)} %bitcast.136) | data formatting | bytes 37748736 | tf_op jit(solution)/shard_map/reshape | solution.py:20
  1085.0 18.7 %copy.188 = f32[3,32,128,384]{3,2,1,0:T(8,128)} copy(f32[3,32,128,384]{2,3,1,0:T(8,128)} %bitcast.135) | data formatting | bytes 37748736 | tf_op jit(solution)/shard_map/reshape | solution.py:20
  1103.7 24.5 %fusion.25 = f32[3,32,128,3,384]{4,2,3,1,0:T(8,128)} fusion(bf16[3,32,128,3,128]{2,4,3,1,0:T(8,128)(2,1)} %bitcast.128, bf16[128,128]{0,1:T(8,128)(2,1)S(1)} %bitcast.155, bf16[128,128]{0,1:T(8,128)(2,1)S(1)} %bitcast.153, bf16[128,128]{0,1:T(8,128)(2,1)S(1)} %bitcast.151), kind=kOutput, calls=%fused_computation.49 | convolution fusion | flops 3624173568 | bytes 66158592 | tf_op jit(solution)/shard_map/dot_general | solution.py:12
  1128.2 9.1 fusion.34
  1137.3 14.4 %fusion.33 = (f32[3,32,128,2,128]{4,2,3,1,0:T(8,128)S(1)}, f32[3,32,128,2,128]{4,2,3,1,0:T(8,128)}) fusion(f32[3,32,128,3,384]{4,2,3,1,0:T(8,128)} %fusion.25), kind=kLoop, calls=%fused_computation.71 | loop fusion | bytes 50331648 | tf_op jit(solution)/shard_map/jit(_roll_static)/slice | solution.py:19
  1151.7 19.5 %fusion.6 = f32[3,32,128,3,128]{4,2,3,1,0:T(8,128)} fusion(f32[3,32,128,3,384]{4,2,3,1,0:T(8,128)} %fusion.25, f32[3,32,128,2,128]{4,2,3,1,0:T(8,128)} %get-tuple-element.16, f32[3,32,128,1,128]{4,2,3,1,0:T(8,128)} %get-tuple-element.18, f32[3,32,128,1,128]{4,2,3,1,0:T(8,128)S(1)} %get-tuple-element.17, f32[3,32,128,2,128]{4,2,3,1,0:T(8,128)S(1)} %get-tuple-element.15), kind=kLoop, calls=%fused_computation.11 | loop fusion | flops 18874368 | bytes 75497472 | tf_op jit(solution)/shard_map/add | solution.py:19
  1171.2 18.6 %copy.193 = f32[3,32,128,3,128]{2,4,3,1,0:T(8,128)} copy(f32[3,32,128,3,128]{4,2,3,1,0:T(8,128)} %fusion.6) | data formatting | bytes 37748736 | tf_op jit(solution)/shard_map/add | solution.py:19
  1189.8 13.1 fusion.11
  1202.9 6.8 copy.194
  1209.7 5.3 fusion.12
  1215.0 6.6 copy.187
  1221.6 11.6 convert_bitcast_fusion.1
  1233.2 15.7 %copy.213 = f32[3,2,16,128,384]{4,3,2,1,0:T(8,128)} copy(f32[3,2,16,128,384]{4,2,0,3,1:T(8,128)} %convert_bitcast_fusion.1) | data formatting | bytes 37748736 | tf_op jit(solution)/shard_map/convert_element_type | solution.py:104
  1249.0 0.8 slice_bitcast_fusion.2
  1249.9 33.5 %all_gather.3 = bf16[2,49152]{1,0:T(2,128)(2,1)S(1)} all-gather(bf16[2,3072]{1,0:T(2,128)(2,1)S(1)} %pad_maximum_fusion.3), channel_id=1, replica_groups=mesh['row'=16,'col'=2] {'row'}, dimensions={1}, use_global_device_ids=true | all-gather | bytes 208896 | tf_op jit(solution)/shard_map/all_gather | solution.py:87
  1283.5 0.3 fusion.21
  1284.5 3.7 multiply_add_fusion
  1288.2 8.9 convert_bitcast_fusion
  1297.1 13.2 copy.204
  1310.3 20.5 %reshape.90 = f32[3,32,128,384]{3,2,1,0:T(8,128)} reshape(f32[3,32,16,3072]{3,2,1,0:T(8,128)} %copy.204) | data formatting | bytes 37748736 | tf_op jit(solution)/shard_map/convert_element_type | solution.py:104
  1330.8 34.6 %add_convert_fusion = bf16[3,32,128,384]{3,2,1,0:T(8,128)(2,1)} fusion(f32[3,32,128,384]{3,2,1,0:T(8,128)} %copy.189, f32[3,32,128,384]{3,2,1,0:T(8,128)} %copy.188, f32[3,32,128,384]{3,2,1,0:T(8,128)} %reshape.90, f32[3,32,128,384]{3,2,1,0:T(8,128)} %bitcast.137, f32[32,128,384]{2,1,0:T(8,128)} %multiply_add_fusion, f32[32,128,384]{2,1,0:T(8,128)} %copy.194, ...), kind=kLoop, calls=%fused_computation.24 | loop fusion | flops 51904512 | bytes 103809040 | tf_op jit(solution)/shard_map/convert_element_type | solution.py:113
  (71 shorter events, 1.7 us)
Async XLA Ops:
  9.1 109.4 %all-to-all-start.3 = ((bf16[3,32,128,384]{3,2,0,1:T(8,128)(2,1)}), bf16[3,32,128,384]{3,2,0,1:T(8,128)(2,1)}, u32[]{:S(2)}, u32[]{:S(2)}) async-start(bf16[3,32,128,384]{3,2,0,1:T(8,128)(2,1)} %copy.205), calls=%async_computation.3 | async-start | bytes 18874368 | tf_op jit(solution)/shard_map/all_to_all | solution.py:95
  118.5 125.8 %all-to-all-start.4 = ((bf16[3,32,128,384]{2,3,0,1:T(8,128)(2,1)}), bf16[3,32,128,384]{2,3,0,1:T(8,128)(2,1)}, u32[]{:S(2)}, u32[]{:S(2)}) async-start(bf16[3,32,128,384]{2,3,0,1:T(8,128)(2,1)} %copy.207), calls=%async_computation.4 | async-start | bytes 18874368 | tf_op jit(solution)/shard_map/all_to_all | solution.py:94
  244.3 210.4 %all-to-all-start.1 = ((bf16[16,2,147456]{2,1,0:T(2,128)(2,1)}), bf16[16,2,147456]{2,1,0:T(2,128)(2,1)}, u32[]{:S(2)}, u32[]{:S(2)}) async-start(bf16[16,2,147456]{2,1,0:T(2,128)(2,1)} %reshape.104), calls=%async_computation.1 | async-start | bytes 18874368 | tf_op jit(solution)/shard_map/all_to_all | solution.py:77
  454.7 326.3 %all-to-all-start = ((bf16[16,2,147456]{2,1,0:T(2,128)(2,1)}), bf16[16,2,147456]{2,1,0:T(2,128)(2,1)}, u32[]{:S(2)}, u32[]{:S(2)}) async-start(bf16[16,2,147456]{2,1,0:T(2,128)(2,1)} %reshape.102), calls=%async_computation | async-start | bytes 18874368 | tf_op jit(solution)/shard_map/all_to_all | solution.py:78
  462.3 12.7 copy-start.9
  462.3 13.1 copy-start.10
  475.2 42.2 %copy-start.2 = (bf16[1,128,128]{1,2,0:T(8,128)(2,1)}, bf16[1,128,128]{1,2,0:T(8,128)(2,1)S(1)}, u32[]{:S(2)}) copy-start(bf16[1,128,128]{1,2,0:T(8,128)(2,1)S(1)} %copy.239) | copy-start | bytes 98308
  475.3 42.1 %copy-start.4 = (bf16[1,128,128]{1,2,0:T(8,128)(2,1)}, bf16[1,128,128]{1,2,0:T(8,128)(2,1)S(1)}, u32[]{:S(2)}) copy-start(bf16[1,128,128]{1,2,0:T(8,128)(2,1)S(1)} %copy.240) | copy-start | bytes 98308
  475.4 41.9 %copy-start.6 = (bf16[1,128,128]{1,2,0:T(8,128)(2,1)}, bf16[1,128,128]{1,2,0:T(8,128)(2,1)S(1)}, u32[]{:S(2)}) copy-start(bf16[1,128,128]{1,2,0:T(8,128)(2,1)S(1)} %copy.241) | copy-start | bytes 98308
  570.6 5.7 copy-start.1
  576.3 12.7 copy-start.8
  576.3 31.4 %slice-start.3 = ((s8[6291456]{0:T(1024)(128)(4,1)}), s8[2097152]{0:T(1024)(128)(4,1)S(1)}, s32[]{:S(2)}) async-start(s8[6291456]{0:T(1024)(128)(4,1)} %bitcast.145), calls=%async_computation.9 | async-start | bytes 4194304
  589.1 18.7 %slice-start.4 = ((s8[6291456]{0:T(1024)(128)(4,1)}), s8[4194304]{0:T(1024)(128)(4,1)S(1)}, s32[]{:S(2)}) async-start(s8[6291456]{0:T(1024)(128)(4,1)} %bitcast.145), calls=%async_computation.10 | async-start | bytes 8388608
  781.0 212.6 %all-to-all-start.5 = ((bf16[3,16,256,384]{3,1,0,2:T(8,128)(2,1)}), bf16[3,16,256,384]{3,1,0,2:T(8,128)(2,1)}, u32[]{:S(2)}, u32[]{:S(2)}) async-start(bf16[3,16,256,384]{3,1,0,2:T(8,128)(2,1)} %copy.212), calls=%async_computation.5 | async-start | bytes 18874368 | tf_op jit(solution)/shard_map/all_to_all | solution.py:103
  882.8 9.2 slice-start
  882.8 9.2 copy-start
  882.8 9.2 slice-start.1
  885.6 6.3 slice-start.2
  903.9 13.1 copy-start.13
  917.0 20.5 %copy-start.12 = (f32[3]{0:T(128)S(1)}, f32[3]{0:T(128)}, u32[]{:S(2)}) copy-start(f32[3]{0:T(128)} %compare_convert_fusion.1) | copy-start | bytes 40
  993.6 294.6 %all-to-all-start.2 = ((bf16[3,512,3072]{2,0,1:T(4,128)(2,1)}), bf16[3,512,3072]{2,0,1:T(4,128)(2,1)}, u32[]{:S(2)}, u32[]{:S(2)}) async-start(bf16[3,512,3072]{2,0,1:T(4,128)(2,1)} %copy.203), calls=%async_computation.2 | async-start | bytes 25165824 | tf_op jit(solution)/shard_map/all_to_all | solution.py:90
  1085.0 18.7 %copy-start.3 = (bf16[1,128,128]{1,2,0:T(8,128)(2,1)S(1)}, bf16[1,128,128]{1,2,0:T(8,128)(2,1)}, u32[]{:S(2)}) copy-start(bf16[1,128,128]{1,2,0:T(8,128)(2,1)} %copy-done.2) | copy-start | bytes 98308
  1085.0 18.7 %copy-start.5 = (bf16[1,128,128]{1,2,0:T(8,128)(2,1)S(1)}, bf16[1,128,128]{1,2,0:T(8,128)(2,1)}, u32[]{:S(2)}) copy-start(bf16[1,128,128]{1,2,0:T(8,128)(2,1)} %copy-done.4) | copy-start | bytes 98308
  1085.0 18.7 %copy-start.7 = (bf16[1,128,128]{1,2,0:T(8,128)(2,1)S(1)}, bf16[1,128,128]{1,2,0:T(8,128)(2,1)}, u32[]{:S(2)}) copy-start(bf16[1,128,128]{1,2,0:T(8,128)(2,1)} %copy-done.6) | copy-start | bytes 98308
  1209.7 11.9 copy-start.11
where the time goes:
time: 1380 us; the launch traced here: 1370 us
  local copies, waits for them, and re-layouts  768 us (56%)
  other arithmetic  215 us (16%)
  waiting for transfers between devices  173 us (13%)
  matrix products  130 us (9%)
  starting transfers between devices  45.1 us (3%)
  blocking collectives  33.5 us (2%)
    unnamed x58, local copies, waits for them, and re-layouts  241 us
    all_to_all x1, waiting for transfers between devices, per_device(): lax.all_to_all(flat_speed, 'row', split_axis=2, concat_axis=1, tiled=True)  118 us
    all_to_all x2, local copies, waits for them, and re-layouts, per_device(): lax.all_to_all(flat_speed, 'row', split_axis=2, concat_axis=1, tiled=True)  106 us
    reshape x1, local copies, waits for them, and re-layouts, per_device(): flat_speed = velocity.reshape(3, local_rows, local_planes * stream_cells)  81.2 us
    slice x6, local copies, waits for them, and re-layouts, along_stream(): jnp.roll(upper, -1, axis=-2)  71 us
    add x3, other arithmetic, along_stream(): jnp.roll(lower, 1, axis=-2) + middle + jnp.roll(upper, -1, axis=-2)  69.8 us
    dot_general x3, matrix products, along_stream(): product = jnp.dot(tiles, joined, preferred_element_type=jnp.float32)  65.7 us
    all_to_all x1, local copies, waits for them, and re-layouts, per_device(): lax.all_to_all(flat_adjoint, 'row', split_axis=2, concat_axis=1, tiled=True)  58.5 us
  transfers between devices with their start and end apart: 6, of which 2 were waited for; matrix products, arithmetic and copies ran while one was open for 75% of the time, Pallas kernels for 0%

commit v1 on v0

--- a/solution.py
+++ b/solution.py
@@ -74,7 +74,12 @@
     flat_speed = velocity.reshape(3, local_rows, local_planes * stream_cells)
     flat_adjoint = adjoint_velocity.reshape(3, local_rows, local_planes * stream_cells)
     speed_lines, adjoint_lines = (
-        lax.all_to_all(flat_speed, "row", split_axis=2, concat_axis=1, tiled=True),
+        jnp.concatenate(
+            jax.lax.all_to_all(
+                jnp.stack(jnp.split(flat_speed, jax.lax.axis_size("row"), 2), 0), "row", 0, 0
+            ),
+            1,
+        ),
         lax.all_to_all(flat_adjoint, "row", split_axis=2, concat_axis=1, tiled=True),
     )
     normal_speed, normal_adjoint, normal_curve = normal_products(

time: 1380 us -> 1230 us (0.89)
  local copies, waits for them, and re-layouts: 768 us -> 571 us
  waiting for transfers between devices: 173 us -> 217 us
    all_to_all x1, waiting for transfers between devices: 0.01 us -> 146 us  [per_device(): lax.all_to_all(flat_adjoint, 'row', split_axis=2, concat_axis=1, tiled=True)]
    all_to_all x1, waiting for transfers between devices: 118 us -> 0.01 us  [per_device(): jax.lax.all_to_all(jnp.stack(jnp.split(flat_speed, jax.lax.axis_size('row...]
    all_to_all x2 -> x0, local copies, waits for them, and re-layouts: 106 us -> none  [per_device(): lax.all_to_all(flat_speed, 'row', split_axis=2, concat_axis=1, tiled=True)]
    reshape x1, local copies, waits for them, and re-layouts: 81.2 us -> 13.1 us  [per_device(): flat_speed = velocity.reshape(3, local_rows, local_planes * stream_cells)]
    unnamed x58 -> x71, local copies, waits for them, and re-layouts: 241 us -> 197 us
    all_to_all x1, waiting for transfers between devices: 0.01 us -> 16.1 us  [per_device(): lax.all_to_all(velocity, 'col', split_axis=1, concat_axis=2, tiled=True)]
  transfers between devices with their start and end apart: 6 -> 6, of which waited for: 2 -> 3; matrix products, arithmetic and copies ran while one was open for 75% -> 68% of each run, Pallas kernels for 0% -> 0%
where the time goes in v1:
time: 1230 us; the launch traced here: 1220 us
  local copies, waits for them, and re-layouts  571 us (46%)
  waiting for transfers between devices  217 us (18%)
  other arithmetic  214 us (17%)
  matrix products  133 us (11%)
  starting transfers between devices  46.7 us (4%)
  blocking collectives  33.5 us (3%)
    unnamed x71, local copies, waits for them, and re-layouts  197 us
    all_to_all x1, waiting for transfers between devices, per_device(): lax.all_to_all(flat_adjoint, 'row', split_axis=2, concat_axis=1, tiled=True)  146 us
    slice x6, local copies, waits for them, and re-layouts, along_stream(): jnp.roll(upper, -1, axis=-2)  71 us
    add x3, other arithmetic, along_stream(): jnp.roll(lower, 1, axis=-2) + middle + jnp.roll(upper, -1, axis=-2)  69.8 us
    dot_general x3, matrix products, along_stream(): product = jnp.dot(tiles, joined, preferred_element_type=jnp.float32)  65.7 us
    all_to_all x1, local copies, waits for them, and re-layouts, per_device(): lax.all_to_all(flat_adjoint, 'row', split_axis=2, concat_axis=1, tiled=True)  58.5 us
    all_to_all x1, waiting for transfers between devices, per_device(): lax.all_to_all(adjoint_velocity, 'col', split_axis=1, concat_axis=2, tile...  55 us
    convert_element_type x1, local copies, waits for them, and re-layouts, per_device(): normal_term = adjoint_terms(speed_lines, adjoint_lines, normal_speed, nor...  39.2 us
  transfers between devices with their start and end apart: 6, of which 3 were waited for; matrix products, arithmetic and copies ran while one was open for 68% of the time, Pallas kernels for 0%

profile of v1, /device:TPU:13, one launch (start us, length us, event | category | flops | bytes accessed | tf_op | source)
XLA Modules:
  0.0 1216.8 jit_solution(10696782658706508443)
XLA Ops:
  0.0 9.1 copy.224
  9.1 7.5 all-to-all-start.3
  16.6 12.6 %copy.208 = bf16[3,32,128,384]{2,3,1,0:T(8,128)(2,1)} copy(bf16[3,32,128,384]{3,2,1,0:T(8,128)(2,1)} %param.12) | data formatting | bytes 18874368 | tf_op args[1]
  29.2 12.6 %copy.207 = bf16[3,32,128,384]{2,3,1,0:T(8,128)(2,1)} copy(bf16[3,32,128,384]{3,2,1,0:T(8,128)(2,1)} %param.11) | data formatting | bytes 18874368 | tf_op args[0]
  42.5 12.5 %add_convert_fusion.2 = bf16[3,32,128,384]{2,3,1,0:T(8,128)(2,1)} fusion(bf16[3,32,128,384]{2,3,1,0:T(8,128)(2,1)} %copy.208, bf16[3,32,128,384]{2,3,1,0:T(8,128)(2,1)} %copy.207, f32[]{:T(128)} %bitcast.187), kind=kLoop, calls=%fused_computation.26 | loop fusion | flops 23592960 | bytes 28311556 | tf_op jit(solution)/shard_map/convert_element_type | solution.py:65
  55.0 8.5 copy.226
  63.5 55.0 %all-to-all-done.3 = bf16[3,32,128,384]{3,2,0,1:T(8,128)(2,1)} async-done(((bf16[3,32,128,384]{3,2,0,1:T(8,128)(2,1)}), bf16[3,32,128,384]{3,2,0,1:T(8,128)(2,1)}, u32[]{:S(2)}, u32[]{:S(2)}) %all-to-all-start.3) | async-done | bytes 9437216 | tf_op jit(solution)/shard_map/all_to_all | solution.py:100
  118.5 8.5 all-to-all-start.4
  127.0 48.7 %copy.217 = bf16[3,32,128,384]{1,0,3,2:T(4,128)(2,1)} copy(bf16[3,32,128,384]{3,2,1,0:T(8,128)(2,1)} %param.13) | data formatting | bytes 18874368 | tf_op args[2]
  175.7 36.1 %reshape.110 = bf16[16,2,147456]{2,1,0:T(2,128)(2,1)} reshape(bf16[49152,3,32]{2,1,0:T(4,128)(2,1)} %bitcast.190) | data formatting | bytes 18874368
  211.7 16.1 %all-to-all-done.4 = bf16[3,32,128,384]{2,3,0,1:T(8,128)(2,1)} async-done(((bf16[3,32,128,384]{2,3,0,1:T(8,128)(2,1)}), bf16[3,32,128,384]{2,3,0,1:T(8,128)(2,1)}, u32[]{:S(2)}, u32[]{:S(2)}) %all-to-all-start.4) | async-done | bytes 9437216 | tf_op jit(solution)/shard_map/all_to_all | solution.py:99
  227.9 8.1 all-to-all-start
  236.0 12.7 %copy.220 = bf16[3,32,128,384]{3,2,1,0:T(8,128)(2,1)} copy(bf16[3,32,128,384]{2,3,1,0:T(8,128)(2,1)} %add_convert_fusion.2) | data formatting | bytes 18874368 | tf_op jit(solution)/shard_map/convert_element_type | solution.py:65
  248.7 13.1 %reshape.93 = bf16[3,32,49152]{2,1,0:T(8,128)(2,1)} reshape(bf16[3,32,128,384]{3,2,1,0:T(8,128)(2,1)} %copy.220) | data formatting | bytes 18874368 | tf_op jit(solution)/shard_map/reshape | solution.py:74
  269.4 2.0 fusion.26
  271.4 2.0 fusion.25
  283.0 2.0 fusion.19
  284.9 2.0 fusion.18
  292.7 145.9 %all-to-all-done = bf16[16,2,147456]{2,1,0:T(2,128)(2,1)} async-done(((bf16[16,2,147456]{2,1,0:T(2,128)(2,1)}), bf16[16,2,147456]{2,1,0:T(2,128)(2,1)}, u32[]{:S(2)}, u32[]{:S(2)}) %all-to-all-start) | async-done | bytes 9437216 | tf_op jit(solution)/shard_map/all_to_all | solution.py:83
  438.6 7.4 all-to-all-start.1
  446.1 12.7 %copy.205 = bf16[3,32,128,384]{2,3,1,0:T(8,128)(2,1)} copy(bf16[3,32,128,384]{3,2,1,0:T(8,128)(2,1)} %param.13) | data formatting | bytes 18874368 | tf_op args[2]
  460.1 40.9 %convolution_bitcast_fusion = f32[3,32,128,3,768]{2,4,3,1,0:T(8,128)} fusion(bf16[3,32,128,3,128]{2,4,3,1,0:T(8,128)(2,1)} %bitcast.191, bf16[128,768]{0,1:T(8,128)(2,1)S(1)} %constant_dynamic-update-slice_fusion), kind=kOutput, calls=%fused_computation | convolution fusion | flops 7247757312 | bytes 122880000 | tf_op jit(solution)/shard_map/dot_general | solution.py:12
  501.1 31.5 %fusion.47 = (f32[3,32,128,2,128]{2,4,3,1,0:T(8,128)}, f32[3,32,128,2,128]{2,4,3,1,0:T(8,128)}, f32[3,32,128,2,128]{2,4,3,1,0:T(8,128)}, f32[3,32,128,2,128]{2,4,3,1,0:T(8,128)}) fusion(f32[3,32,128,3,768]{2,4,3,1,0:T(8,128)} %convolution_bitcast_fusion), kind=kLoop, calls=%fused_computation.101 | loop fusion | bytes 100663296 | tf_op jit(solution)/shard_map/jit(_roll_static)/slice | solution.py:19
  532.6 9.1 copy.225
  541.7 12.6 %copy.228 = bf16[3,2,16,128,384]{4,3,1,2,0:T(8,128)(2,1)} copy(bf16[3,2,16,128,384]{3,4,0,2,1:T(8,128)(2,1)} %bitcast.54) | data formatting | bytes 18874368 | tf_op jit(solution)/shard_map/all_to_all | solution.py:99
  554.4 2.4 slice.220
  556.8 3.3 convert.21
  560.1 12.7 %fusion.9 = f32[16,256,384]{2,1,0:T(8,128)} fusion(bf16[3,16,256,384]{3,2,1,0:T(8,128)(2,1)} %bitcast.192, bf16[3,16,256,384]{3,2,1,0:T(8,128)(2,1)} %bitcast.198, bf16[256,256]{1,0:T(8,128)(2,1)S(1)} %copy-done.1), kind=kOutput, calls=%fused_computation.18 | convolution fusion | flops 2428502016 | bytes 25296896 | tf_op jit(solution)/shard_map/vz,cyzx->cyvx/dot_general | solution.py:33
  572.8 18.7 %convolution_bitcast_fusion.2 = f32[3,16,512,384]{3,2,1,0:T(8,128)} fusion(bf16[3,16,256,384]{3,2,1,0:T(8,128)(2,1)} %bitcast.193, bf16[256,256]{1,0:T(8,128)(2,1)S(1)} %copy-done.8, bf16[256,256]{1,0:T(8,128)(2,1)S(1)} %copy-done.1), kind=kOutput, calls=%fused_computation.28 | convolution fusion | flops 4832362496 | bytes 47448064 | tf_op jit(solution)/shard_map/vz,cyzx->cyvx/dot_general | solution.py:35
  591.5 19.2 %fusion.2 = bf16[3,16,256,384]{3,2,1,0:T(8,128)(2,1)} fusion(f32[3,16,512,384]{3,2,1,0:T(8,128)} %convolution_bitcast_fusion.2, f32[16,256,384]{2,1,0:T(8,128)} %fusion.9, f32[3]{0:T(128)S(1)} %compare_convert_fusion, f32[16,256,384]{2,1,0:T(8,128)S(1)} %bitcast.204), kind=kLoop, calls=%fused_computation.5 | loop fusion | flops 23592960 | bytes 59768844 | tf_op jit(solution)/shard_map/convert_element_type | solution.py:107
  610.7 12.8 %copy.231 = bf16[3,16,256,384]{3,1,0,2:T(8,128)(2,1)} copy(bf16[3,16,256,384]{3,2,1,0:T(8,128)(2,1)} %fusion.2) | data formatting | bytes 18874368 | tf_op jit(solution)/shard_map/convert_element_type | solution.py:107
  623.5 35.8 %reshape.111 = bf16[49152,3,32]{2,1,0:T(4,128)(2,1)} reshape(bf16[16,2,147456]{2,1,0:T(2,128)(2,1)} %all-to-all-done) | data formatting | bytes 18874368
  659.4 58.5 %copy.250 = bf16[3,32,16,3072]{3,1,2,0:T(8,128)(2,1)} copy(bf16[3,32,16,3072]{1,0,3,2:T(4,128)(2,1)} %bitcast.189) | data formatting | bytes 18874368 | tf_op jit(solution)/shard_map/all_to_all | solution.py:83
  717.8 8.9 all-to-all-start.5
  726.7 8.8 copy.221
  735.6 15.8 %bitcast_convert_fusion = (bf16[3,512,3072]{2,1,0:T(8,128)(2,1)}, f32[3,3072,512]{1,2,0:T(8,128)}) fusion(bf16[3,512,3072]{2,1,0:T(8,128)(2,1)} %bitcast.202, bf16[512,512]{1,0:T(8,128)(2,1)S(1)} %copy-done), kind=kOutput, calls=%fused_computation.19 | convolution fusion | flops 4836556800 | bytes 38273024 | tf_op jit(solution)/shard_map/wy,cyp->cwp/dot_general | solution.py:25
  751.4 11.2 fusion.10
  762.6 2.2 slice.217
  764.9 3.6 bitcast_convert_fusion.1
  768.5 20.1 %convolution_bitcast_fusion.1 = f32[3,1024,3072]{2,1,0:T(8,128)} fusion(bf16[3,512,3072]{2,1,0:T(8,128)(2,1)} %bitcast.199, bf16[512,512]{1,0:T(8,128)(2,1)S(1)} %copy-done.13, bf16[512,512]{1,0:T(8,128)(2,1)S(1)} %copy-done), kind=kOutput, calls=%fused_computation.27 | convolution fusion | flops 9665773568 | bytes 48234496 | tf_op jit(solution)/shard_map/wy,cyp->cwp/dot_general | solution.py:27
  788.6 16.9 %fusion.5 = bf16[3,512,3072]{2,1,0:T(8,128)(2,1)S(1)} fusion(f32[3,1024,3072]{2,1,0:T(8,128)} %convolution_bitcast_fusion.1, f32[512,3072]{1,0:T(8,128)} %fusion.10, f32[3]{0:T(128)S(1)} %copy-done.12, f32[512,3072]{1,0:T(8,128)} %bitcast_convert_fusion.1), kind=kLoop, calls=%fused_computation.9 | loop fusion | flops 23592960 | bytes 59768844 | tf_op jit(solution)/shard_map/convert_element_type | solution.py:90
  805.5 39.2 %copy.222 = bf16[3,512,3072]{2,0,1:T(4,128)(2,1)} copy(bf16[3,512,3072]{2,1,0:T(8,128)(2,1)S(1)} %fusion.5) | data formatting | bytes 18874368 | tf_op jit(solution)/shard_map/convert_element_type | solution.py:90
  844.7 6.3 all-to-all-start.2
  851.0 16.0 %fusion.48 = (f32[3,32,128,1,128]{2,4,3,1,0:T(8,128)}, f32[3,32,128,1,128]{2,4,3,1,0:T(8,128)}, f32[3,32,128,1,128]{2,4,3,1,0:T(8,128)}, f32[3,32,128,1,128]{2,4,3,1,0:T(8,128)}) fusion(f32[3,32,128,3,768]{2,4,3,1,0:T(8,128)} %convolution_bitcast_fusion), kind=kLoop, calls=%fused_computation.102 | loop fusion | bytes 50331648 | tf_op jit(solution)/shard_map/jit(_roll_static)/slice | solution.py:19
  867.0 50.3 %fusion.7 = (f32[3,32,128,3,128]{2,4,3,1,0:T(8,128)}, f32[3,32,128,3,128]{2,4,3,1,0:T(8,128)}) fusion(f32[3,32,128,3,768]{2,4,3,1,0:T(8,128)} %convolution_bitcast_fusion, f32[3,32,128,2,128]{2,4,3,1,0:T(8,128)} %get-tuple-element.8, f32[3,32,128,1,128]{2,4,3,1,0:T(8,128)} %get-tuple-element.12, f32[3,32,128,1,128]{2,4,3,1,0:T(8,128)} %get-tuple-element.11, ...), kind=kLoop, calls=%fused_computation.13 | loop fusion | flops 37748736 | bytes 150994944 | tf_op jit(solution)/shard_map/add | solution.py:19
  917.2 18.7 %copy.211 = f32[3,32,128,384]{3,2,1,0:T(8,128)} copy(f32[3,32,128,384]{2,3,1,0:T(8,128)} %bitcast.195) | data formatting | bytes 37748736 | tf_op jit(solution)/shard_map/reshape | solution.py:20
  935.9 18.7 %copy.210 = f32[3,32,128,384]{3,2,1,0:T(8,128)} copy(f32[3,32,128,384]{2,3,1,0:T(8,128)} %bitcast.194) | data formatting | bytes 37748736 | tf_op jit(solution)/shard_map/reshape | solution.py:20
  954.6 24.5 %fusion.41 = f32[3,32,128,3,384]{4,2,3,1,0:T(8,128)} fusion(bf16[3,32,128,3,128]{2,4,3,1,0:T(8,128)(2,1)} %bitcast.188, bf16[128,128]{0,1:T(8,128)(2,1)S(1)} %bitcast.212, bf16[128,128]{0,1:T(8,128)(2,1)S(1)} %bitcast.210, bf16[128,128]{0,1:T(8,128)(2,1)S(1)} %bitcast.208), kind=kOutput, calls=%fused_computation.81 | convolution fusion | flops 3624173568 | bytes 66158592 | tf_op jit(solution)/shard_map/dot_general | solution.py:12
  979.1 9.1 fusion.50
  988.2 14.4 %fusion.49 = (f32[3,32,128,2,128]{4,2,3,1,0:T(8,128)S(1)}, f32[3,32,128,2,128]{4,2,3,1,0:T(8,128)}) fusion(f32[3,32,128,3,384]{4,2,3,1,0:T(8,128)} %fusion.41), kind=kLoop, calls=%fused_computation.103 | loop fusion | bytes 50331648 | tf_op jit(solution)/shard_map/jit(_roll_static)/slice | solution.py:19
  1002.6 19.5 %fusion.6 = f32[3,32,128,3,128]{4,2,3,1,0:T(8,128)} fusion(f32[3,32,128,3,384]{4,2,3,1,0:T(8,128)} %fusion.41, f32[3,32,128,2,128]{4,2,3,1,0:T(8,128)} %get-tuple-element.16, f32[3,32,128,1,128]{4,2,3,1,0:T(8,128)} %get-tuple-element.18, f32[3,32,128,1,128]{4,2,3,1,0:T(8,128)S(1)} %get-tuple-element.17, f32[3,32,128,2,128]{4,2,3,1,0:T(8,128)S(1)} %get-tuple-element.15), kind=kLoop, calls=%fused_computation.11 | loop fusion | flops 18874368 | bytes 75497472 | tf_op jit(solution)/shard_map/add | solution.py:19
  1022.1 18.6 %copy.215 = f32[3,32,128,3,128]{2,4,3,1,0:T(8,128)} copy(f32[3,32,128,3,128]{4,2,3,1,0:T(8,128)} %fusion.6) | data formatting | bytes 37748736 | tf_op jit(solution)/shard_map/add | solution.py:19
  1040.7 13.1 %fusion.11 = f32[32,128,384]{1,2,0:T(8,128)} fusion(f32[3,32,128,3,128]{2,4,3,1,0:T(8,128)} %copy.215, bf16[3,32,128,384]{2,3,1,0:T(8,128)(2,1)} %copy.205), kind=kLoop, calls=%fused_computation.23 | loop fusion | flops 12582912 | bytes 34603008 | tf_op jit(solution)/shard_map/reduce_sum | solution.py:45
  1053.8 6.8 copy.216
  1060.6 5.3 fusion.12
  1066.0 6.6 copy.209
  1072.5 11.6 convert_bitcast_fusion.1
  1084.2 15.7 %copy.232 = f32[3,2,16,128,384]{4,3,2,1,0:T(8,128)} copy(f32[3,2,16,128,384]{4,2,0,3,1:T(8,128)} %convert_bitcast_fusion.1) | data formatting | bytes 37748736 | tf_op jit(solution)/shard_map/convert_element_type | solution.py:109
  1100.8 33.5 %all_gather.3 = bf16[2,49152]{1,0:T(2,128)(2,1)S(1)} all-gather(bf16[2,3072]{1,0:T(2,128)(2,1)S(1)} %pad_maximum_fusion.3), channel_id=1, replica_groups=mesh['row'=16,'col'=2] {'row'}, dimensions={1}, use_global_device_ids=true | all-gather | bytes 208896 | tf_op jit(solution)/shard_map/all_gather | solution.py:92
  1135.5 3.7 multiply_add_fusion
  1139.2 8.9 convert_bitcast_fusion
  1148.1 13.2 %copy.223 = f32[3,32,16,3072]{3,2,1,0:T(8,128)} copy(f32[3,32,16,3072]{3,0,1,2:T(4,128)S(1)} %convert_bitcast_fusion) | data formatting | bytes 37748736 | tf_op jit(solution)/shard_map/convert_element_type | solution.py:109
  1161.3 20.5 %reshape.98 = f32[3,32,128,384]{3,2,1,0:T(8,128)} reshape(f32[3,32,16,3072]{3,2,1,0:T(8,128)} %copy.223) | data formatting | bytes 37748736 | tf_op jit(solution)/shard_map/convert_element_type | solution.py:109
  1181.7 34.6 %add_convert_fusion = bf16[3,32,128,384]{3,2,1,0:T(8,128)(2,1)} fusion(f32[3,32,128,384]{3,2,1,0:T(8,128)} %copy.211, f32[3,32,128,384]{3,2,1,0:T(8,128)} %copy.210, f32[3,32,128,384]{3,2,1,0:T(8,128)} %reshape.98, f32[3,32,128,384]{3,2,1,0:T(8,128)} %bitcast.196, f32[32,128,384]{2,1,0:T(8,128)} %multiply_add_fusion, f32[32,128,384]{2,1,0:T(8,128)} %copy.216, ...), kind=kLoop, calls=%fused_computation.24 | loop fusion | flops 51904512 | bytes 103809040 | tf_op jit(solution)/shard_map/convert_element_type | solution.py:118
  (85 shorter events, 26.4 us)
Async XLA Ops:
  9.1 109.4 %all-to-all-start.3 = ((bf16[3,32,128,384]{3,2,0,1:T(8,128)(2,1)}), bf16[3,32,128,384]{3,2,0,1:T(8,128)(2,1)}, u32[]{:S(2)}, u32[]{:S(2)}) async-start(bf16[3,32,128,384]{3,2,0,1:T(8,128)(2,1)} %copy.224), calls=%async_computation.3 | async-start | bytes 18874368 | tf_op jit(solution)/shard_map/all_to_all | solution.py:100
  118.5 109.4 %all-to-all-start.4 = ((bf16[3,32,128,384]{2,3,0,1:T(8,128)(2,1)}), bf16[3,32,128,384]{2,3,0,1:T(8,128)(2,1)}, u32[]{:S(2)}, u32[]{:S(2)}) async-start(bf16[3,32,128,384]{2,3,0,1:T(8,128)(2,1)} %copy.226), calls=%async_computation.4 | async-start | bytes 18874368 | tf_op jit(solution)/shard_map/all_to_all | solution.py:99
  227.9 210.8 %all-to-all-start = ((bf16[16,2,147456]{2,1,0:T(2,128)(2,1)}), bf16[16,2,147456]{2,1,0:T(2,128)(2,1)}, u32[]{:S(2)}, u32[]{:S(2)}) async-start(bf16[16,2,147456]{2,1,0:T(2,128)(2,1)} %reshape.110), calls=%async_computation | async-start | bytes 18874368 | tf_op jit(solution)/shard_map/all_to_all | solution.py:83
  438.6 279.2 %all-to-all-start.1 = ((bf16[16,3,32,3072]{3,2,1,0:T(8,128)(2,1)}), bf16[16,3,32,3072]{3,2,1,0:T(8,128)(2,1)}, u32[]{:S(2)}, u32[]{:S(2)}) async-start(bf16[16,3,32,3072]{3,2,1,0:T(8,128)(2,1)} %fusion.15), calls=%async_computation.1 | async-start | bytes 18874368 | tf_op jit(solution)/shard_map/all_to_all | solution.py:78
  446.1 12.7 %copy-start.9 = (bf16[3,128,128]{2,1,0:T(8,128)(2,1)S(1)}, bf16[3,128,128]{2,1,0:T(8,128)(2,1)}, u32[]{:S(2)}) copy-start(bf16[3,128,128]{2,1,0:T(8,128)(2,1)} %param.15) | copy-start | bytes 294916
  446.1 13.1 %copy-start.10 = (bf16[3,128,128]{2,1,0:T(8,128)(2,1)S(1)}, bf16[3,128,128]{2,1,0:T(8,128)(2,1)}, u32[]{:S(2)}) copy-start(bf16[3,128,128]{2,1,0:T(8,128)(2,1)} %param.16) | copy-start | bytes 294916
  458.9 42.2 %copy-start.2 = (bf16[1,128,128]{1,2,0:T(8,128)(2,1)}, bf16[1,128,128]{1,2,0:T(8,128)(2,1)S(1)}, u32[]{:S(2)}) copy-start(bf16[1,128,128]{1,2,0:T(8,128)(2,1)S(1)} %copy.254) | copy-start | bytes 98308
  459.0 42.1 %copy-start.4 = (bf16[1,128,128]{1,2,0:T(8,128)(2,1)}, bf16[1,128,128]{1,2,0:T(8,128)(2,1)S(1)}, u32[]{:S(2)}) copy-start(bf16[1,128,128]{1,2,0:T(8,128)(2,1)S(1)} %copy.255) | copy-start | bytes 98308
  459.1 41.9 %copy-start.6 = (bf16[1,128,128]{1,2,0:T(8,128)(2,1)}, bf16[1,128,128]{1,2,0:T(8,128)(2,1)S(1)}, u32[]{:S(2)}) copy-start(bf16[1,128,128]{1,2,0:T(8,128)(2,1)S(1)} %copy.256) | copy-start | bytes 98308
  554.3 5.7 copy-start.1
  560.1 12.7 %copy-start.8 = (bf16[256,256]{1,0:T(8,128)(2,1)S(1)}, bf16[256,256]{1,0:T(8,128)(2,1)}, u32[]{:S(2)}) copy-start(bf16[256,256]{1,0:T(8,128)(2,1)} %param.20) | copy-start | bytes 393220
  560.1 31.4 %slice-start.3 = ((s8[6291456]{0:T(1024)(128)(4,1)}), s8[2097152]{0:T(1024)(128)(4,1)S(1)}, s32[]{:S(2)}) async-start(s8[6291456]{0:T(1024)(128)(4,1)} %bitcast.203), calls=%async_computation.9 | async-start | bytes 4194304
  572.8 18.7 %slice-start.4 = ((s8[6291456]{0:T(1024)(128)(4,1)}), s8[4194304]{0:T(1024)(128)(4,1)S(1)}, s32[]{:S(2)}) async-start(s8[6291456]{0:T(1024)(128)(4,1)} %bitcast.203), calls=%async_computation.10 | async-start | bytes 8388608
  717.8 126.9 %all-to-all-start.5 = ((bf16[3,16,256,384]{3,1,0,2:T(8,128)(2,1)}), bf16[3,16,256,384]{3,1,0,2:T(8,128)(2,1)}, u32[]{:S(2)}, u32[]{:S(2)}) async-start(bf16[3,16,256,384]{3,1,0,2:T(8,128)(2,1)} %copy.231), calls=%async_computation.5 | async-start | bytes 18874368 | tf_op jit(solution)/shard_map/all_to_all | solution.py:108
  726.7 8.9 copy-start
  726.7 24.7 %slice-start = ((s8[9437184]{0:T(1024)(128)(4,1)}), s8[1048576]{0:T(1024)(128)(4,1)S(1)}, s32[]{:S(2)}) async-start(s8[9437184]{0:T(1024)(128)(4,1)} %bitcast.200), calls=%async_computation.6 | async-start | bytes 2097152
  735.6 15.8 %slice-start.1 = ((s8[9437184]{0:T(1024)(128)(4,1)}), s8[4194304]{0:T(1024)(128)(4,1)S(1)}, s32[]{:S(2)}) async-start(s8[9437184]{0:T(1024)(128)(4,1)} %bitcast.200), calls=%async_computation.7 | async-start | bytes 8388608
  735.6 15.8 %slice-start.2 = ((s8[9437184]{0:T(1024)(128)(4,1)}), s8[4194304]{0:T(1024)(128)(4,1)S(1)}, s32[]{:S(2)}) async-start(s8[9437184]{0:T(1024)(128)(4,1)} %bitcast.200), calls=%async_computation.8 | async-start | bytes 8388608
  762.6 5.9 copy-start.13
  768.5 20.1 %copy-start.12 = (f32[3]{0:T(128)S(1)}, f32[3]{0:T(128)}, u32[]{:S(2)}) copy-start(f32[3]{0:T(128)} %compare_convert_fusion.1) | copy-start | bytes 40
  844.7 294.5 %all-to-all-start.2 = ((bf16[3,512,3072]{2,0,1:T(4,128)(2,1)}), bf16[3,512,3072]{2,0,1:T(4,128)(2,1)}, u32[]{:S(2)}, u32[]{:S(2)}) async-start(bf16[3,512,3072]{2,0,1:T(4,128)(2,1)} %copy.222), calls=%async_computation.2 | async-start | bytes 25165824 | tf_op jit(solution)/shard_map/all_to_all | solution.py:95
  935.9 18.7 %copy-start.3 = (bf16[1,128,128]{1,2,0:T(8,128)(2,1)S(1)}, bf16[1,128,128]{1,2,0:T(8,128)(2,1)}, u32[]{:S(2)}) copy-start(bf16[1,128,128]{1,2,0:T(8,128)(2,1)} %copy-done.2) | copy-start | bytes 98308
  935.9 18.7 %copy-start.5 = (bf16[1,128,128]{1,2,0:T(8,128)(2,1)S(1)}, bf16[1,128,128]{1,2,0:T(8,128)(2,1)}, u32[]{:S(2)}) copy-start(bf16[1,128,128]{1,2,0:T(8,128)(2,1)} %copy-done.4) | copy-start | bytes 98308
  935.9 18.7 %copy-start.7 = (bf16[1,128,128]{1,2,0:T(8,128)(2,1)S(1)}, bf16[1,128,128]{1,2,0:T(8,128)(2,1)}, u32[]{:S(2)}) copy-start(bf16[1,128,128]{1,2,0:T(8,128)(2,1)} %copy-done.6) | copy-start | bytes 98308
  1060.6 11.9 copy-start.11
